TPU v7x, 32 devices: a whole 2x2x4 slice. The times are simulated.
32 devices in a mesh: grp: 2 (over core), dev: 16 (over z, y, x).
Axes of the slice: x: 2, y: 2, z: 4, core: 2. Of those that a mesh axis runs over, the one named last changes fastest.
Arguments:
- queries: float32 [32, 12, 128], P(('grp', 'dev')), may hold values from -2.1 to 2.1
- pages: float32 [32, 256, 128], P(('grp', 'dev')), may hold values from -2.1 to 2.1
- positive: int32 [32], replicated, may hold values from 0 to 31
Outputs:
- loss: float32 [], replicated
- question_token_slope: float32 [32, 12, 128], P(('grp', 'dev'))
- page_grad: float32 [32, 256, 128], P(('grp', 'dev'))
All inputs are finite; a program needn't handle non-finite values.
Results may differ from a plain program's by a relative error of at most 0.00019.
Values sent between devices are 32-bit elements; how exact they have to be, the bound alone decides.
A program may use at most 64 MiB of HBM per device.

v0:
```python
import jax
import jax.numpy as jnp
from jax import lax
from jax.sharding import PartitionSpec as P

cap_value = 4.0
sharpness_divisor = 0.25
logit_scale = 8.0
z_weight = 0.001
highest = lax.Precision.HIGHEST


def block_partial_terms(query_rows, page_rows, query_tokens):
    scores = jnp.dot(query_rows, page_rows.T, precision=highest, preferred_element_type=jnp.float32)
    tangent = jnp.tanh(scores / cap_value)
    bounded_similarity = cap_value * tangent
    exponential_grid = jnp.exp(bounded_similarity / sharpness_divisor)
    accumulated_totals = jnp.sum(exponential_grid, axis=1)
    gentle_peak = sharpness_divisor * jnp.log(accumulated_totals)
    slopes = (
        exponential_grid
        / accumulated_totals[:, None]
        * (1.0 - tangent * tangent)
        * (logit_scale / query_tokens)
    )
    return (gentle_peak, slopes)


def shards(queries, pages, positive):
    gathered = lax.all_gather(queries, ("grp", "dev"), axis=0, tiled=True)
    query_count, query_tokens, feature_width = gathered.shape
    page_rows = pages[0]
    page_index = lax.axis_index(("grp", "dev"))
    block_size = 16
    block_count = query_count // block_size
    query_blocks = gathered.reshape(block_count, block_size * query_tokens, feature_width)
    chosen = (positive == page_index).astype(jnp.float32)

    def block_logits(gentle_peak):
        return (
            logit_scale / query_tokens * gentle_peak.reshape(block_size, query_tokens).sum(axis=1)
        )

    def evaluate_loss_and_slopes(query_rows):
        gentle_peak, slopes = block_partial_terms(query_rows, page_rows, query_tokens)
        unscaled = jnp.dot(slopes, page_rows, precision=highest, preferred_element_type=jnp.float32)
        return (block_logits(gentle_peak), unscaled)

    logits, unscaled = lax.map(evaluate_loss_and_slopes, query_blocks)
    statistics_logits = logits.reshape(query_count)
    exponential_grid = jnp.exp(statistics_logits)
    accumulated_totals, matching_logit = lax.psum(
        (exponential_grid, chosen * statistics_logits), ("grp", "dev")
    )
    log_totals = jnp.log(accumulated_totals)
    loss = jnp.mean(log_totals - matching_logit + z_weight * log_totals * log_totals)
    coefficients = (
        (1.0 + 2.0 * z_weight * log_totals) * exponential_grid / accumulated_totals - chosen
    ) / query_count
    loss, coefficients = (loss, coefficients)
    factors = jnp.repeat(coefficients, query_tokens).reshape(
        block_count, block_size * query_tokens, 1
    )
    query_terms = unscaled * factors

    def page_only(page_total, inputs):
        query_rows, factor_rows = inputs
        unused_smooth, slopes = block_partial_terms(query_rows, page_rows, query_tokens)
        token_grads = slopes * factor_rows
        page_total = page_total + jnp.dot(
            token_grads.T, query_rows, precision=highest, preferred_element_type=jnp.float32
        )
        return (page_total, None)

    page_start = jnp.zeros(page_rows.shape, jnp.float32)
    page_total, unused_outputs = lax.scan(page_only, page_start, (query_blocks, factors))
    query_terms = query_terms.reshape(query_count, query_tokens, feature_width)
    summed = lax.psum(query_terms, ("grp", "dev"))
    own_count = queries.shape[0]
    question_token_slope = lax.dynamic_slice_in_dim(summed, page_index * own_count, own_count, 0)
    return (loss, question_token_slope, page_total[None])


def solution(mesh):
    return jax.shard_map(
        shards,
        mesh=mesh,
        in_specs=(P(("grp", "dev"), None, None), P(("grp", "dev"), None, None), P()),
        out_specs=(P(), P(("grp", "dev"), None, None), P(("grp", "dev"), None, None)),
        check_vma=False,
    )
```

profile of v0, /device:TPU:0, one launch (start us, length us, event | category | flops | bytes accessed | tf_op | source)
XLA Modules:
  0.0 258.3 jit_solution(4730078051259543547)
XLA Ops:
  7.2 0.0 all-reduce.3.cloned.1.call-start
  7.2 0.0 copy-start.1
  7.2 0.7 copy-done.1
  7.9 71.4 %all_gather.3 = f32[32,12,128]{2,1,0:T(8,128)S(1)} all-gather(f32[1,12,128]{2,1,0:T(8,128)S(1)} %copy.13), channel_id=1, replica_groups=mesh['grp'=2,'dev'=16] {'grp','dev'}, dimensions={0}, use_global_device_ids=true | all-gather | bytes 202752 | tf_op jit(solution)/shard_map/all_gather | solution.py:30
  79.3 0.0 copy-start
  79.3 0.9 copy-done
  80.2 2.2 while.27
  80.2 0.4 fusion.57
  80.7 0.4 fusion.58
  81.1 0.1 mul.190
  81.2 0.1 reduce_sum.54
  81.3 0.4 fusion.57
  81.8 0.4 fusion.58
  82.2 0.1 mul.190
  82.3 0.1 reduce_sum.54
  82.5 0.1 reshape.46
  82.5 0.0 copy-start.2
  82.5 0.7 copy-done.2
  83.2 36.8 %all-reduce = (f32[32]{0:T(128)S(1)}, f32[32]{0:T(128)S(1)}) all-reduce(f32[32]{0:T(128)S(1)} %get-tuple-element.208, f32[32]{0:T(128)S(1)} %get-tuple-element.207), channel_id=1, replica_groups=mesh['grp'=2,'dev'=16] {'grp','dev'}, use_global_device_ids=true, to_apply=%region_5.6 | all-reduce | flops 64 | bytes 512 | tf_op jit(solution)/shard_map/psum | solution.py:52
  120.0 0.6 fusion.39
  120.6 0.1 broadcast_in_dim.34
  120.7 0.1 broadcast_in_dim.35
  120.7 0.1 broadcast_in_dim.36
  120.8 0.1 broadcast_multiply_fusion
  121.0 0.7 reshape.47
  121.7 0.0 all-reduce.3.cloned.1.call-update
  121.7 0.1 broadcast_in_dim.40
  121.8 2.5 while.28
  121.8 0.4 fusion.62
  122.3 0.8 convolution_add_fusion.2
  123.1 0.4 fusion.62
  123.5 0.8 convolution_add_fusion.2
  124.3 0.0 copy-start.3
  125.0 124.0 %all-reduce.3.cloned.1.call-done = f32[32,12,128]{2,1,0:T(8,128)} async-done(((f32[32,12,128]{2,1,0:T(8,128)}), f32[32,12,128]{2,1,0:T(8,128)}) %all-reduce.3.cloned.1.call-update) | async-done | bytes 196624 | tf_op jit(solution)/shard_map/psum | solution.py:78
  249.0 0.7 constant_dynamic-slice_fusion
  249.7 0.6 copy.15
  250.3 0.0 copy-done.3
  (14 shorter events, 0.1 us)
Async XLA Ops:
  7.2 241.8 %all-reduce.3.cloned.1.call-start = ((), (), s32[]{:S(2)}) async-start(), calls=%async_computation | async-start | bytes 524288 | tf_op jit(solution)/shard_map/psum | solution.py:78
  7.2 0.7 copy-start.1
  79.3 0.9 copy-start
  82.5 0.7 copy-start.2
  124.3 126.0 %copy-start.3 = (f32[256,128]{1,0:T(8,128)}, f32[256,128]{1,0:T(8,128)S(1)}, u32[]{:S(2)}) copy-start(f32[256,128]{1,0:T(8,128)S(1)} %get-tuple-element.136) | copy-start | bytes 393220
Sparse Core Ops, SparseCore 0:
  121.8 127.1 all-reduce.2
where the time goes:
time: 259 us; the launch traced here: 258 us
  waiting for transfers between devices  124 us (48%)
  blocking collectives  108 us (42%)
  between operations  15.9 us (6%)
  local copies, waits for them, and re-layouts  4.91 us (2%)
  matrix products  4.08 us (2%)
    psum x1, waiting for transfers between devices, shards(): summed = lax.psum(query_terms, ('grp', 'dev'))  124 us
    all_gather x1, blocking collectives, shards(): gathered = lax.all_gather(queries, ('grp', 'dev'), axis=0, tiled=True)  71.4 us
    psum x1, blocking collectives, shards(): lax.psum((exponential_grid, chosen * statistics_logits), ('grp', 'dev'))  36.8 us
  transfers between devices with their start and end apart: 1, of which 1 were waited for; matrix products, arithmetic and copies ran while one was open for 1% of the time, Pallas kernels for 0%

commit v1 on v0

--- a/solution.py
+++ b/solution.py
@@ -75,7 +75,7 @@
     page_start = jnp.zeros(page_rows.shape, jnp.float32)
     page_total, unused_outputs = lax.scan(page_only, page_start, (query_blocks, factors))
     query_terms = query_terms.reshape(query_count, query_tokens, feature_width)
-    summed = lax.psum(query_terms, ("grp", "dev"))
+    summed = jnp.sum(lax.all_gather(query_terms, ("grp", "dev")), axis=0)
     own_count = queries.shape[0]
     question_token_slope = lax.dynamic_slice_in_dim(summed, page_index * own_count, own_count, 0)
     return (loss, question_token_slope, page_total[None])

time: 259 us -> 206 us (0.80)
  waiting for transfers between devices: 124 us -> 64.7 us
  matrix products: 4.08 us -> 9.5 us
  other arithmetic: 1.01 us -> 4.41 us
    psum x1 -> x0, waiting for transfers between devices: 124 us -> none  [shards(): summed = lax.psum(query_terms, ('grp', 'dev'))]
    all_gather x0 -> x1, waiting for transfers between devices: none -> 64.7 us  [shards(): summed = jnp.sum(lax.all_gather(query_terms, ('grp', 'dev')), axis=0)]
    dot_general x4, matrix products: 1.79 us -> 5.41 us  [block_partial_terms(): jnp.dot(query_rows, page_rows.T, precision=highest, preferred_element_typ...]
    reduce_sum x0 -> x1, other arithmetic: none -> 3.4 us  [shards(): summed = jnp.sum(lax.all_gather(query_terms, ('grp', 'dev')), axis=0)]
  transfers between devices with their start and end apart: 1 -> 1, of which waited for: 1 -> 1; matrix products, arithmetic and copies ran while one was open for 1% -> 2% of each run, Pallas kernels for 0% -> 0%
where the time goes in v1:
time: 206 us
  blocking collectives  108 us (52%)
  waiting for transfers between devices  64.7 us (31%)
  between operations  15.9 us (8%)
  matrix products  9.5 us (5%)
  other arithmetic  4.41 us (2%)
  local copies, waits for them, and re-layouts  2.74 us (1%)
    all_gather x1, blocking collectives, shards(): gathered = lax.all_gather(queries, ('grp', 'dev'), axis=0, tiled=True)  71.4 us
    all_gather x1, waiting for transfers between devices, shards(): summed = jnp.sum(lax.all_gather(query_terms, ('grp', 'dev')), axis=0)  64.7 us
    psum x1, blocking collectives, shards(): lax.psum((exponential_grid, chosen * statistics_logits), ('grp', 'dev'))  36.8 us
    dot_general x4, matrix products, block_partial_terms(): jnp.dot(query_rows, page_rows.T, precision=highest, preferred_element_typ...  5.41 us
  transfers between devices with their start and end apart: 1, of which 1 were waited for; matrix products, arithmetic and copies ran while one was open for 2% of the time, Pallas kernels for 0%

profile of v1, /device:TPU:0, one launch (start us, length us, event | category | flops | bytes accessed | tf_op | source)
XLA Modules:
  0.0 205.7 jit_solution(10949903801709902702)
XLA Ops:
  7.2 0.0 copy-start
  7.2 0.0 all-gather.2.cloned.1.call-start
  7.2 0.7 copy.14
  7.9 71.4 %all_gather.6 = f32[32,12,128]{2,1,0:T(8,128)S(1)} all-gather(f32[1,12,128]{2,1,0:T(8,128)S(1)} %copy.14), channel_id=1, replica_groups=mesh['grp'=2,'dev'=16] {'grp','dev'}, dimensions={0}, use_global_device_ids=true | all-gather | bytes 202752 | tf_op jit(solution)/shard_map/all_gather | solution.py:30
  79.4 5.8 %while.27 = (s32[]{:T(128)}, f32[2,16]{1,0:T(2,128)S(1)}, f32[2,192,128]{2,1,0:T(8,128)S(1)}, f32[2,192,128]{2,1,0:T(8,128)S(1)}, f32[256,128]{1,0:T(8,128)}, /*index=5*/s32[]{:T(128)}, f32[]{:T(128)}, s32[]{:T(128)}) while((s32[]{:T(128)}, f32[2,16]{1,0:T(2,128)S(1)}, f32[2,192,128]{2,1,0:T(8,128)S(1)}, f32[2,192,128]{2,1,0:T(8,128)S(1)}, ...), condition=%wide.region_3.4_spmd, body=%wide.region_0.3_spmd.sunk | while | flops 151437504 | bytes 858029 | solution.py:49
  79.4 1.4 fusion.57
  80.7 1.3 fusion.58
  82.0 0.1 mul.190
  82.1 0.1 reduce_sum.64
  82.3 1.4 fusion.57
  83.6 1.3 fusion.58
  85.0 0.1 mul.190
  85.0 0.1 reduce_sum.64
  85.2 0.1 reshape.43
  85.3 0.0 copy-done
  85.3 36.8 %all-reduce = (f32[32]{0:T(128)S(1)}, f32[32]{0:T(128)S(1)}) all-reduce(f32[32]{0:T(128)S(1)} %get-tuple-element.205, f32[32]{0:T(128)S(1)} %get-tuple-element.204), channel_id=1, replica_groups=mesh['grp'=2,'dev'=16] {'grp','dev'}, use_global_device_ids=true, to_apply=%region_5.6 | all-reduce | flops 64 | bytes 512 | tf_op jit(solution)/shard_map/psum | solution.py:52
  122.1 0.6 fusion.39
  122.7 0.1 broadcast_in_dim.34
  122.8 0.1 broadcast_in_dim.35
  122.9 0.1 broadcast_in_dim.36
  123.0 0.1 broadcast_multiply_fusion
  123.1 0.7 copy.15
  123.9 0.0 all-gather.2.cloned.1.call-update
  123.9 0.1 broadcast_in_dim.40
  124.7 4.3 %while.28 = (s32[]{:T(128)}, f32[256,128]{1,0:T(8,128)S(1)}, f32[2,192,128]{2,1,0:T(8,128)S(1)}, f32[256,128]{1,0:T(8,128)}, f32[2,192,1]{1,2,0:T(1,128)S(1)}, /*index=5*/s32[]{:T(128)}, s32[]{:T(128)}) while((s32[]{:T(128)}, f32[256,128]{1,0:T(8,128)S(1)}, f32[2,192,128]{2,1,0:T(8,128)S(1)}, f32[256,128]{1,0:T(8,128)}, ...), condition=%wide.region_10.11_spmd.clone, body=%wide.region_8.10_spmd.clone.sunk | while | flops 151502848 | bytes 987499 | solution.py:76
  124.7 1.4 fusion.62
  126.0 0.8 convolution_add_fusion.2
  126.9 1.4 fusion.62
  128.2 0.8 convolution_add_fusion.2
  129.0 0.0 copy-start.1
  129.0 64.7 %all-gather.2.cloned.1.call-done = f32[32,32,12,128]{3,1,2,0:T(8,128)} async-done(((f32[1,32,12,128]{3,1,2,0:T(8,128)}), f32[32,32,12,128]{3,1,2,0:T(8,128)}) %all-gather.2.cloned.1.call-update) | async-done | bytes 6291472 | tf_op jit(solution)/shard_map/all_gather | solution.py:78
  193.7 3.4 %reduce_sum.55 = f32[32,12,128]{2,0,1:T(8,128)S(1)} reduce(f32[32,32,12,128]{3,1,2,0:T(8,128)} %all-gather.2.cloned.1.call-done, f32[]{:T(128)} %constant.120.clone.1), dimensions={0}, to_apply=%region_7.8 | reduce | flops 1523712 | bytes 6488068 | tf_op jit(solution)/shard_map/reduce_sum | solution.py:78
  197.1 0.6 constant_dynamic-slice_fusion
  197.7 0.0 copy-done.1
  (14 shorter events, 0.2 us)
Async XLA Ops:
  7.2 78.1 %copy-start = (s32[32]{0:T(128)S(1)}, s32[32]{0:T(128)}, u32[]{:S(2)}) copy-start(s32[32]{0:T(128)} %param.9) | copy-start | bytes 388
  7.2 186.6 %all-gather.2.cloned.1.call-start = ((), (), s32[]{:S(2)}) async-start(), calls=%async_computation | async-start | bytes 6488064 | tf_op jit(solution)/shard_map/all_gather | solution.py:78
  129.0 68.7 %copy-start.1 = (f32[256,128]{1,0:T(8,128)}, f32[256,128]{1,0:T(8,128)S(1)}, u32[]{:S(2)}) copy-start(f32[256,128]{1,0:T(8,128)S(1)} %get-tuple-element.136) | copy-start | bytes 393220
Sparse Core Ops, SparseCore 0:
  124.0 69.6 all-gather.1
